TPU v7x, 512 devices: a whole 4x4x16 slice. The times are simulated.
512 devices in a mesh: gx: 32 (over y, z_hi, core), gy: 16 (over z_lo, x).
Axes of the slice: x: 4, y: 4, z: 16 (z_hi: 4, z_lo: 4; z = z_hi * 4 + z_lo), core: 2. Of those that a mesh axis runs over, the one named last changes fastest.
Arguments:
- gradient: float32 [2, 16, 512, 2048], P(None, None, 'gx', 'gy'), may hold values from -6 to 6
- corr_length: float32 [2, 3], replicated, may hold values from 1 to 16, as said below
- scale: float32 [2, 16, 512, 2048], P(None, None, 'gx', 'gy'), may hold values from 0.25 to 4
- w_first: bfloat16 [16, 2, 3, 3, 3], replicated, may hold values from -0.875 to 0.875
- b_first: float32 [16], replicated, may hold values from -3 to 3
- w_middle: bfloat16 [16, 16, 3, 3, 3], replicated, may hold values from -0.3125 to 0.3125
- b_middle: float32 [16], replicated, may hold values from -3 to 3
- w_last: bfloat16 [2, 16, 3, 3, 3], replicated, may hold values from -0.3125 to 0.3125
- b_last: float32 [2], replicated, may hold values from -3 to 3
Outputs:
- update: float32 [2, 16, 512, 2048], P(None, None, 'gx', 'gy')
Inputs may be any that keep to these rules, and one draw needn't show every extreme that they name: corr_length[:, 0] and corr_length[:, 1] lie between 6 and 16; corr_length[:, 2] lies between 1 and 2.5.
All inputs are finite; a program needn't handle non-finite values.
Results may differ from a plain program's by a relative error of at most 0.0021.
Values may be sent and summed in bfloat16 or wider, within the bound.
A program may use at most 64 MiB of HBM per device.

v0:
```python
import math

import jax
import jax.numpy as jnp
from jax import lax
from jax.sharding import PartitionSpec as P

RAD = 16


def with_halo(cells, sides, width):
    for axis, dim in sides:
        count = lax.axis_size(axis)
        ends = count - 1
        head = lax.slice_in_dim(cells, 0, width, axis=dim)
        tail = lax.slice_in_dim(cells, cells.shape[dim] - width, cells.shape[dim], axis=dim)
        cells = jnp.concatenate(
            [
                lax.ppermute(tail, axis, [(i, (i + 1) % count) for i in range(ends)]),
                cells,
                lax.ppermute(head, axis, [((i + 1) % count, i) for i in range(ends)]),
            ],
            axis=dim,
        )
    return cells


def taps_of(length):
    reach = jnp.arange(-RAD, RAD + 1).astype(jnp.float32)
    scaled_r = math.sqrt(3.0) * jnp.abs(reach)[None, :] / length[:, None]
    values = (1.0 + scaled_r) * jnp.exp(-scaled_r)
    return values / jnp.sqrt(jnp.sum(values * values, axis=1, keepdims=True))


def band_matrix(taps, rows_in, rows_out, offset):
    diff = jnp.arange(rows_in)[:, None] - jnp.arange(rows_out)[None, :] + offset
    onehot = (diff[:, :, None] == jnp.arange(2 * RAD + 1)[None, None, :]).astype(jnp.float32)
    return jnp.einsum("wxk,fk->fwx", onehot, taps, precision=lax.Precision.HIGHEST)


def conv_rows(field, kernel):
    depth = field.shape[1]
    rows_out = field.shape[2] - 2
    cols_out = field.shape[3] - 2
    padded = jnp.pad(field, ((0, 0), (1, 1), (0, 0), (0, 0)))

    def one_row(index):
        slab = lax.dynamic_slice_in_dim(padded, index, 3, 2)
        stacked = jnp.stack([slab[:, level : level + depth] for level in range(3)], axis=1)
        total = jnp.zeros((kernel.shape[0], depth, cols_out), jnp.float32)
        for shift in range(3):
            total = total + jnp.einsum(
                "ocab,cazby->ozy",
                kernel[:, :, :, :, shift],
                stacked[:, :, :, :, shift : shift + cols_out],
                preferred_element_type=jnp.float32,
            )
        return total

    rows = lax.map(one_row, jnp.arange(rows_out))
    return jnp.moveaxis(rows, 0, 2)


def widen(field):
    return with_halo(field, (("gx", 2), ("gy", 3)), 1)


def per_device(gradient, corr_length, scale, w_first, b_first, w_middle, b_middle, w_last, b_last):
    depth = gradient.shape[1]
    cells_x = gradient.shape[2]
    cells_y = gradient.shape[3]
    taps_x = taps_of(corr_length[:, 0])
    taps_y = taps_of(corr_length[:, 1])
    taps_z = taps_of(corr_length[:, 2])
    band_x = band_matrix(taps_x, cells_x + 2 * RAD, cells_x, 0)
    band_y = band_matrix(taps_y, cells_y + 2 * RAD, cells_y, 0)
    band_z = band_matrix(taps_z, depth, depth, RAD)
    highest = lax.Precision.HIGHEST
    wide_x = with_halo(gradient, (("gx", 2),), RAD)
    along_x = jnp.einsum("fzwy,fwx->fzxy", wide_x, band_x, precision=highest)
    wide_y = with_halo(along_x, (("gy", 3),), RAD)
    along_y = jnp.einsum("fzxw,fwy->fzxy", wide_y, band_y, precision=highest)
    smoothed = jnp.einsum("fwxy,fwz->fzxy", along_y, band_z, precision=highest)
    scaled = scale * smoothed
    net_in = scaled.astype(jnp.bfloat16)
    hidden = jax.nn.silu(conv_rows(widen(net_in), w_first) + b_first[:, None, None, None]).astype(
        jnp.bfloat16
    )
    hidden = jax.nn.silu(conv_rows(widen(hidden), w_middle) + b_middle[:, None, None, None]).astype(
        jnp.bfloat16
    )
    correction = conv_rows(widen(hidden), w_last) + b_last[:, None, None, None]
    return scaled + correction


def solution(mesh):
    return jax.shard_map(
        per_device,
        mesh=mesh,
        in_specs=(
            P(None, None, "gx", "gy"),
            P(),
            P(None, None, "gx", "gy"),
            P(),
            P(),
            P(),
            P(),
            P(),
            P(),
        ),
        out_specs=P(None, None, "gx", "gy"),
        check_vma=False,
    )
```

profile of v0, /device:TPU:47, one launch (start us, length us, event | category | flops | bytes accessed | tf_op | source)
XLA Modules:
  0.0 343.5 jit_solution(1066386968489439752)
XLA Ops:
  0.0 9.4 %collective-permute-start = (f32[2,16,16,128]{3,2,1,0:T(8,128)}, f32[2,16,16,128]{3,2,1,0:T(8,128)S(1)}, u32[]{:S(2)}, u32[]{:S(2)}) collective-permute-start(f32[2,16,16,128]{3,2,1,0:T(8,128)} %param.15), channel_id=1, source_target_pairs={{0,16},{16,32},{32,48},{48,64},{64,80},{80,96},{96,112},{112,128},... | collective-permute-start | bytes 786440 | tf_op jit(solution)/shard_map/ppermute | solution.py:19
  14.1 2.4 collective-permute-done
  16.5 13.2 %collective-permute-done.1 = f32[2,16,16,128]{3,2,1,0:T(8,128)S(1)} collective-permute-done((f32[2,16,16,128]{3,2,1,0:T(8,128)}, f32[2,16,16,128]{3,2,1,0:T(8,128)S(1)}, u32[]{:S(2)}, u32[]{:S(2)}) %collective-permute-start.1) | collective-permute-done | bytes 262176 | tf_op jit(solution)/shard_map/ppermute | solution.py:21
  33.2 3.4 collective-permute-start.3
  38.7 3.7 %collective-permute-done.3 = f32[2,16,16,16]{3,2,1,0:T(8,128)S(1)} collective-permute-done((f32[2,16,16,16]{3,2,1,0:T(8,128)S(1)}, f32[2,16,16,16]{3,2,1,0:T(8,128)S(1)}, u32[]{:S(2)}, u32[]{:S(2)}) %collective-permute-start.3) | collective-permute-done | bytes 32800 | tf_op jit(solution)/shard_map/ppermute | solution.py:21
  44.8 3.0 collective-permute-start.4
  49.7 6.9 %collective-permute-done.5 = bf16[2,16,1,128]{3,1,2,0:T(8,128)(2,1)S(1)} collective-permute-done((bf16[2,16,1,128]{3,1,2,0:T(8,128)(2,1)S(1)}, bf16[2,16,1,128]{3,1,2,0:T(8,128)(2,1)S(1)}, u32[]{:S(2)}, u32[]{:S(2)}) %collective-permute-start.5) | collective-permute-done | bytes 8224 | tf_op jit(solution)/shard_map/ppermute | solution.py:21
  58.7 3.4 collective-permute-start.7
  62.7 4.0 %collective-permute-done.7 = bf16[2,16,18,1]{3,1,2,0:T(8,128)(2,1)S(1)} collective-permute-done((bf16[2,16,18,1]{3,1,2,0:T(8,128)(2,1)S(1)}, bf16[2,16,18,1]{3,1,2,0:T(8,128)(2,1)S(1)}, u32[]{:S(2)}, u32[]{:S(2)}) %collective-permute-start.7) | collective-permute-done | bytes 1184 | tf_op jit(solution)/shard_map/ppermute | solution.py:21
  67.4 59.0 %while.30 = (s32[]{:T(128)}, f32[16,16,16,128]{3,2,0,1:T(8,128)S(1)}, s32[16]{0:T(128)S(1)}, bf16[2,18,18,130]{3,1,2,0:T(8,128)(2,1)S(1)}, bf16[16,2,3,3,3]{0,3,...) while((s32[]{:T(128)}, f32[16,16,16,128]{3,2,0,1:T(8,128)S(1)}, ...), condition=%wide.region_4.5_spmd, body=%wide.region_3.4_spmd.sunk | while | flops 3679367 | bytes 1680315 | solution.py:60
  127.1 5.5 %collective-permute-start.8 = (bf16[16,16,1,128]{3,1,2,0:T(8,128)(2,1)S(1)}, bf16[16,16,1,128]{3,1,2,0:T(8,128)(2,1)}, u32[]{:S(2)}, u32[]{:S(2)}) collective-permute-start(bf16[16,16,1,128]{3,1,2,0:T(8,128)(2,1)S(1)} %get-tuple-element.187), channel_id=1, source_target_pairs={{0,16},{16,32},{32,48},{48,64},{64,80},{80,96},{96,112},{112,128},... | collective-permute-start | bytes 196616 | tf_op jit(solution)/shard_map/ppermute | solution.py:19
  134.5 7.7 %collective-permute-done.9 = bf16[16,16,1,128]{3,1,2,0:T(8,128)(2,1)} collective-permute-done((bf16[16,16,1,128]{3,1,2,0:T(8,128)(2,1)S(1)}, bf16[16,16,1,128]{3,1,2,0:T(8,128)(2,1)}, u32[]{:S(2)}, u32[]{:S(2)}) %collective-permute-start.9) | collective-permute-done | bytes 65568 | tf_op jit(solution)/shard_map/ppermute | solution.py:21
  143.8 2.2 copy.101
  149.5 3.5 %collective-permute-start.11 = (bf16[16,16,18,1]{2,1,3,0:T(8,128)(2,1)S(1)}, bf16[16,16,18,1]{2,1,3,0:T(8,128)(2,1)}, u32[]{:S(2)}, u32[]{:S(2)}) collective-permute-start(bf16[16,16,18,1]{2,1,3,0:T(8,128)(2,1)S(1)} %copy.102), channel_id=1, source_target_pairs={{1,0},{2,1},{3,2},{4,3},{5,4},{6,5},{7,6},{8,7},{9,8},{10,9},{11,1... | collective-permute-start | bytes 27656 | tf_op jit(solution)/shard_map/ppermute | solution.py:21
  156.8 2.5 copy.55
  159.3 2.9 pad_maximum_fusion.3
  165.6 77.6 %while.31 = (s32[]{:T(128)}, f32[16,16,16,128]{3,2,0,1:T(8,128)}, s32[16]{0:T(128)S(1)}, bf16[16,18,18,130]{3,0,2,1:T(8,128)(2,1)S(1)}, bf16[16,16,3,3,3]{1,0,3,...) while((s32[]{:T(128)}, f32[16,16,16,128]{3,2,0,1:T(8,128)}, s32[16]{0:T(128)S(1)}, ...), condition=%wide.region_6.7_spmd, body=%wide.region_5.6_spmd.sunk | while | flops 28976136 | bytes 5194423 | solution.py:60
  245.4 4.2 %collective-permute-start.12 = (bf16[16,16,1,128]{3,1,2,0:T(8,128)(2,1)S(1)}, bf16[16,16,1,128]{3,1,2,0:T(8,128)(2,1)S(1)}, u32[]{:S(2)}, u32[]{:S(2)}) collective-permute-start(bf16[16,16,1,128]{3,1,2,0:T(8,128)(2,1)S(1)} %get-tuple-element.185), channel_id=1, source_target_pairs={{0,16},{16,32},{32,48},{48,64},{64,80},{80,96},{96,112},{112,128},... | collective-permute-start | bytes 196616 | tf_op jit(solution)/shard_map/ppermute | solution.py:19
  251.5 8.3 %collective-permute-done.13 = bf16[16,16,1,128]{3,1,2,0:T(8,128)(2,1)S(1)} collective-permute-done((bf16[16,16,1,128]{3,1,2,0:T(8,128)(2,1)S(1)}, bf16[16,16,1,128]{3,1,2,0:T(8,128)(2,1)S(1)}, u32[]{:S(2)}, u32[]{:S(2)}) %collective-permute-start.13) | collective-permute-done | bytes 65568 | tf_op jit(solution)/shard_map/ppermute | solution.py:21
  262.7 3.0 collective-permute-start.14
  267.3 2.5 collective-permute-start.15
  272.2 2.4 collective-permute-done.15
  274.6 2.5 copy.62
  281.5 61.1 %while.32 = (s32[]{:T(128)}, f32[16,2,16,128]{3,2,0,1:T(8,128)S(1)}, s32[16]{0:T(128)S(1)}, bf16[16,18,18,130]{3,0,2,1:T(8,128)(2,1)S(1)}, bf16[2,16,3,3,3]{1,0,...) while((s32[]{:T(128)}, f32[16,2,16,128]{3,2,0,1:T(8,128)S(1)}, s32[16]{0:T(128)S(1)}, ...), condition=%wide.region_8.9_spmd, body=%wide.region_7.8_spmd.sunk | while | flops 4146183 | bytes 4294331 | solution.py:60
  (451 shorter events, 154.0 us)
Async XLA Ops:
  0.0 16.5 %collective-permute-start = (f32[2,16,16,128]{3,2,1,0:T(8,128)}, f32[2,16,16,128]{3,2,1,0:T(8,128)S(1)}, u32[]{:S(2)}, u32[]{:S(2)}) collective-permute-start(f32[2,16,16,128]{3,2,1,0:T(8,128)} %param.15), channel_id=1, source_target_pairs={{0,16},{16,32},{32,48},{48,64},{64,80},{80,96},{96,112},{112,128},... | collective-permute-start | bytes 786440 | tf_op jit(solution)/shard_map/ppermute | solution.py:19
  9.4 20.3 %collective-permute-start.1 = (f32[2,16,16,128]{3,2,1,0:T(8,128)}, f32[2,16,16,128]{3,2,1,0:T(8,128)S(1)}, u32[]{:S(2)}, u32[]{:S(2)}) collective-permute-start(f32[2,16,16,128]{3,2,1,0:T(8,128)} %param.15), channel_id=1, source_target_pairs={{16,0},{32,16},{48,32},{64,48},{80,64},{96,80},{112,96},{128,112},... | collective-permute-start | bytes 786440 | tf_op jit(solution)/shard_map/ppermute | solution.py:21
  14.1 29.5 %copy-start.1 = (f32[2,16,16,128]{3,2,1,0:T(8,128)S(1)}, f32[2,16,16,128]{3,2,1,0:T(8,128)}, u32[]{:S(2)}) copy-start(f32[2,16,16,128]{3,2,1,0:T(8,128)} %param.17) | copy-start | bytes 786436
  31.3 7.4 %collective-permute-start.2 = (f32[2,16,16,16]{3,2,1,0:T(8,128)S(1)}, f32[2,16,16,16]{3,2,1,0:T(8,128)S(1)}, u32[]{:S(2)}, u32[]{:S(2)}) collective-permute-start(f32[2,16,16,16]{3,2,1,0:T(8,128)S(1)} %get-tuple-element.189), channel_id=1, source_target_pairs={{0,1},{1,2},{2,3},{3,4},{4,5},{5,6},{6,7},{7,8},{8,9},{9,10},{10,1... | collective-permute-start | bytes 98312 | tf_op jit(solution)/shard_map/ppermute | solution.py:19
  33.2 9.2 %collective-permute-start.3 = (f32[2,16,16,16]{3,2,1,0:T(8,128)S(1)}, f32[2,16,16,16]{3,2,1,0:T(8,128)S(1)}, u32[]{:S(2)}, u32[]{:S(2)}) collective-permute-start(f32[2,16,16,16]{3,2,1,0:T(8,128)S(1)} %get-tuple-element.190), channel_id=1, source_target_pairs={{1,0},{2,1},{3,2},{4,3},{5,4},{6,5},{7,6},{8,7},{9,8},{10,9},{11,1... | collective-permute-start | bytes 98312 | tf_op jit(solution)/shard_map/ppermute | solution.py:21
  37.2 24.9 %copy-start.5 = (bf16[16,2,3,3,3]{0,1,4,3,2:T(2,128)(2,1)S(1)}, bf16[16,2,3,3,3]{0,1,4,3,2:T(2,128)(2,1)}, u32[]{:S(2)}) copy-start(bf16[16,2,3,3,3]{0,1,4,3,2:T(2,128)(2,1)} %param.18) | copy-start | bytes 5188
  44.8 5.0 %collective-permute-start.4 = (bf16[2,16,1,128]{3,1,2,0:T(8,128)(2,1)S(1)}, bf16[2,16,1,128]{3,1,2,0:T(8,128)(2,1)S(1)}, u32[]{:S(2)}, u32[]{:S(2)}) collective-permute-start(bf16[2,16,1,128]{3,1,2,0:T(8,128)(2,1)S(1)} %get-tuple-element.193), channel_id=1, source_target_pairs={{0,16},{16,32},{32,48},{48,64},{64,80},{80,96},{96,112},{112,128},... | collective-permute-start | bytes 24584 | tf_op jit(solution)/shard_map/ppermute | solution.py:19
  47.8 8.9 %collective-permute-start.5 = (bf16[2,16,1,128]{3,1,2,0:T(8,128)(2,1)S(1)}, bf16[2,16,1,128]{3,1,2,0:T(8,128)(2,1)S(1)}, u32[]{:S(2)}, u32[]{:S(2)}) collective-permute-start(bf16[2,16,1,128]{3,1,2,0:T(8,128)(2,1)S(1)} %get-tuple-element.194), channel_id=1, source_target_pairs={{16,0},{32,16},{48,32},{64,48},{80,64},{96,80},{112,96},{128,112},... | collective-permute-start | bytes 24584 | tf_op jit(solution)/shard_map/ppermute | solution.py:21
  56.8 5.9 %collective-permute-start.6 = (bf16[2,16,18,1]{3,1,2,0:T(8,128)(2,1)S(1)}, bf16[2,16,18,1]{3,1,2,0:T(8,128)(2,1)S(1)}, u32[]{:S(2)}, u32[]{:S(2)}) collective-permute-start(bf16[2,16,18,1]{3,1,2,0:T(8,128)(2,1)S(1)} %get-tuple-element.191), channel_id=1, source_target_pairs={{0,1},{1,2},{2,3},{3,4},{4,5},{5,6},{6,7},{7,8},{8,9},{9,10},{10,1... | collective-permute-start | bytes 3464 | tf_op jit(solution)/shard_map/ppermute | solution.py:19
  58.7 8.0 %collective-permute-start.7 = (bf16[2,16,18,1]{3,1,2,0:T(8,128)(2,1)S(1)}, bf16[2,16,18,1]{3,1,2,0:T(8,128)(2,1)S(1)}, u32[]{:S(2)}, u32[]{:S(2)}) collective-permute-start(bf16[2,16,18,1]{3,1,2,0:T(8,128)(2,1)S(1)} %get-tuple-element.192), channel_id=1, source_target_pairs={{1,0},{2,1},{3,2},{4,3},{5,4},{6,5},{7,6},{8,7},{9,8},{10,9},{11,1... | collective-permute-start | bytes 3464 | tf_op jit(solution)/shard_map/ppermute | solution.py:21
  67.4 59.0 %copy-start.7 = (f32[16]{0:T(128)S(1)}, f32[16]{0:T(128)}, u32[]{:S(2)}) copy-start(f32[16]{0:T(128)} %param.19) | copy-start | bytes 196
  127.1 7.4 %collective-permute-start.8 = (bf16[16,16,1,128]{3,1,2,0:T(8,128)(2,1)S(1)}, bf16[16,16,1,128]{3,1,2,0:T(8,128)(2,1)}, u32[]{:S(2)}, u32[]{:S(2)}) collective-permute-start(bf16[16,16,1,128]{3,1,2,0:T(8,128)(2,1)S(1)} %get-tuple-element.187), channel_id=1, source_target_pairs={{0,16},{16,32},{32,48},{48,64},{64,80},{80,96},{96,112},{112,128},... | collective-permute-start | bytes 196616 | tf_op jit(solution)/shard_map/ppermute | solution.py:19
  132.6 9.6 %collective-permute-start.9 = (bf16[16,16,1,128]{3,1,2,0:T(8,128)(2,1)S(1)}, bf16[16,16,1,128]{3,1,2,0:T(8,128)(2,1)}, u32[]{:S(2)}, u32[]{:S(2)}) collective-permute-start(bf16[16,16,1,128]{3,1,2,0:T(8,128)(2,1)S(1)} %get-tuple-element.188), channel_id=1, source_target_pairs={{16,0},{32,16},{48,32},{64,48},{80,64},{96,80},{112,96},{128,112},... | collective-permute-start | bytes 196616 | tf_op jit(solution)/shard_map/ppermute | solution.py:21
  146.0 8.0 %collective-permute-start.10 = (bf16[16,16,18,1]{2,1,3,0:T(8,128)(2,1)}, bf16[16,16,18,1]{2,1,3,0:T(8,128)(2,1)S(1)}, u32[]{:S(2)}, u32[]{:S(2)}) collective-permute-start(bf16[16,16,18,1]{2,1,3,0:T(8,128)(2,1)} %copy.101), channel_id=1, source_target_pairs={{0,1},{1,2},{2,3},{3,4},{4,5},{5,6},{6,7},{7,8},{8,9},{9,10},{10,1... | collective-permute-start | bytes 27656 | tf_op jit(solution)/shard_map/ppermute | solution.py:19
  149.5 7.2 %collective-permute-start.11 = (bf16[16,16,18,1]{2,1,3,0:T(8,128)(2,1)S(1)}, bf16[16,16,18,1]{2,1,3,0:T(8,128)(2,1)}, u32[]{:S(2)}, u32[]{:S(2)}) collective-permute-start(bf16[16,16,18,1]{2,1,3,0:T(8,128)(2,1)S(1)} %copy.102), channel_id=1, source_target_pairs={{1,0},{2,1},{3,2},{4,3},{5,4},{6,5},{7,6},{8,7},{9,8},{10,9},{11,1... | collective-permute-start | bytes 27656 | tf_op jit(solution)/shard_map/ppermute | solution.py:21
  165.6 77.6 %copy-start.8 = (f32[16]{0:T(128)S(1)}, f32[16]{0:T(128)}, u32[]{:S(2)}) copy-start(f32[16]{0:T(128)} %param.21) | copy-start | bytes 196
  245.4 6.1 %collective-permute-start.12 = (bf16[16,16,1,128]{3,1,2,0:T(8,128)(2,1)S(1)}, bf16[16,16,1,128]{3,1,2,0:T(8,128)(2,1)S(1)}, u32[]{:S(2)}, u32[]{:S(2)}) collective-permute-start(bf16[16,16,1,128]{3,1,2,0:T(8,128)(2,1)S(1)} %get-tuple-element.185), channel_id=1, source_target_pairs={{0,16},{16,32},{32,48},{48,64},{64,80},{80,96},{96,112},{112,128},... | collective-permute-start | bytes 196616 | tf_op jit(solution)/shard_map/ppermute | solution.py:19
  249.6 10.2 %collective-permute-start.13 = (bf16[16,16,1,128]{3,1,2,0:T(8,128)(2,1)S(1)}, bf16[16,16,1,128]{3,1,2,0:T(8,128)(2,1)S(1)}, u32[]{:S(2)}, u32[]{:S(2)}) collective-permute-start(bf16[16,16,1,128]{3,1,2,0:T(8,128)(2,1)S(1)} %get-tuple-element.186), channel_id=1, source_target_pairs={{16,0},{32,16},{48,32},{64,48},{80,64},{96,80},{112,96},{128,112},... | collective-permute-start | bytes 196616 | tf_op jit(solution)/shard_map/ppermute | solution.py:21
  260.5 9.4 %copy-start.3 = (bf16[2,16,3,3,3]{1,0,4,3,2:T(2,128)(2,1)S(1)}, bf16[2,16,3,3,3]{1,0,4,3,2:T(2,128)(2,1)}, u32[]{:S(2)}) copy-start(bf16[2,16,3,3,3]{1,0,4,3,2:T(2,128)(2,1)} %param.22) | copy-start | bytes 5188
  262.7 7.8 %collective-permute-start.14 = (bf16[16,16,18,1]{2,1,3,0:T(8,128)(2,1)}, bf16[16,16,18,1]{2,1,3,0:T(8,128)(2,1)S(1)}, u32[]{:S(2)}, u32[]{:S(2)}) collective-permute-start(bf16[16,16,18,1]{2,1,3,0:T(8,128)(2,1)} %copy.103), channel_id=1, source_target_pairs={{0,1},{1,2},{2,3},{3,4},{4,5},{5,6},{6,7},{7,8},{8,9},{9,10},{10,1... | collective-permute-start | bytes 27656 | tf_op jit(solution)/shard_map/ppermute | solution.py:19
  267.3 7.2 %collective-permute-start.15 = (bf16[16,16,18,1]{2,1,3,0:T(8,128)(2,1)S(1)}, bf16[16,16,18,1]{2,1,3,0:T(8,128)(2,1)}, u32[]{:S(2)}, u32[]{:S(2)}) collective-permute-start(bf16[16,16,18,1]{2,1,3,0:T(8,128)(2,1)S(1)} %copy.104), channel_id=1, source_target_pairs={{1,0},{2,1},{3,2},{4,3},{5,4},{6,5},{7,6},{8,7},{9,8},{10,9},{11,1... | collective-permute-start | bytes 27656 | tf_op jit(solution)/shard_map/ppermute | solution.py:21
  280.5 1.0 copy-start.2
  281.5 61.1 %copy-start = (f32[2,16,16,128]{3,1,2,0:T(8,128)S(1)}, f32[2,16,16,128]{3,1,2,0:T(8,128)}, u32[]{:S(2)}) copy-start(f32[2,16,16,128]{3,1,2,0:T(8,128)} %get-tuple-element.196) | copy-start | bytes 786436
  281.5 61.1 %copy-start.6 = (f32[2]{0:T(128)S(1)}, f32[2]{0:T(128)}, u32[]{:S(2)}) copy-start(f32[2]{0:T(128)} %param.23) | copy-start | bytes 28
  (1 other events, 0.9 us)
where the time goes:
time: 347 us; the launch traced here: 343 us
  loops' own time  92.4 us (27%)
  local copies, waits for them, and re-layouts  73.1 us (21%)
  matrix products  53.1 us (15%)
  waiting for transfers between devices  51.7 us (15%)
  starting transfers between devices  51.2 us (15%)
  other arithmetic  21.4 us (6%)
    another operation x3, loops' own time, conv_rows(): rows = lax.map(one_row, jnp.arange(rows_out))  92.4 us
    dot_general x144, matrix products, one_row(): jnp.einsum('ocab,cazby->ozy', kernel[:, :, :, :, shift], stacked[:, :, :,...  47.6 us
    ppermute x8, waiting for transfers between devices, with_halo(): lax.ppermute(head, axis, [((i + 1) % count, i) for i in range(ends)])  47.3 us
    ppermute x8, starting transfers between devices, with_halo(): lax.ppermute(tail, axis, [(i, (i + 1) % count) for i in range(ends)])  30.7 us
    dynamic_slice x48, local copies, waits for them, and re-layouts, conv_rows(): rows = lax.map(one_row, jnp.arange(rows_out))  28.8 us
    ppermute x8, starting transfers between devices, with_halo(): lax.ppermute(head, axis, [((i + 1) % count, i) for i in range(ends)])  20.5 us
    dynamic_update_slice x48, local copies, waits for them, and re-layouts, conv_rows(): rows = lax.map(one_row, jnp.arange(rows_out))  12.5 us
    another operation x48, other arithmetic, one_row(): jnp.stack([slab[:, level:level + depth] for level in range(3)], axis=1)  11.4 us
  transfers between devices with their start and end apart: 16, of which 11 were waited for; matrix products, arithmetic and copies ran while one was open for 3% of the time, Pallas kernels for 0%

commit v1 on v0

v1 whole, which is shorter than its diff:
```python
import math

import jax
import jax.numpy as jnp
from jax import lax
from jax.experimental import pallas as pl
from jax.experimental.pallas import tpu as pltpu
from jax.sharding import PartitionSpec as P

RAD = 16
RIM = 3
HALO = RAD + RIM
MESH = pl.DeviceIdType.MESH
F32 = jnp.float32
BF16 = jnp.bfloat16
ROWS = 144
ROOT = math.sqrt(3.0)


def iota(shape, dim):
    return lax.broadcasted_iota(jnp.int32, shape, dim)


def dot(a, b):
    return lax.dot_general(a, b, (((1,), (0,)), ((), ())), preferred_element_type=F32)


def split(value):
    high = value.astype(BF16)
    return high, (value - high.astype(F32)).astype(BF16)


def tap(length, distance):
    s = (ROOT * distance.astype(F32)) / length
    return (1.0 + s) * jnp.exp(-s)


def tap_rows(length):
    rows = [tap(length, jnp.full((8, 128), r, jnp.int32)) for r in range(RAD + 1)]
    total = rows[0] * rows[0]
    for row in rows[1:]:
        total = total + 2.0 * (row * row)
    inverse = 1.0 / jnp.sqrt(total)
    return [row * inverse for row in rows], inverse


def silu(v):
    return v / (1.0 + jnp.exp(-v))


def kernel(
    nx, ny, lens, b1s, b2s, b3s, g_ref, s_ref, w1, w2, w3, out_ref,
    gsend, ssend, xl, xr, sl, sr, field, along, scales, pack_l, pack_r, from_l, from_r,
    own_h, own_l, rim_h, rim_l, zmat, smooth, rimscale, scaled, turned, lhs, hid1, hid2, t1, t2, t3,
    send_sem, recv_sem, ysend_sem, yrecv_sem,
):
    gx = lax.axis_index("gx")
    gy = lax.axis_index("gy")
    at = lambda step: {"gx": lax.rem(gx + nx + step, nx)}

    for x in range(16):
        gsend[x] = g_ref[pl.ds(x, 32, stride=16), :].reshape(2, 16, 128).astype(BF16)
    for n, x in enumerate((0, 1, 2, 13, 14, 15)):
        ssend[n] = s_ref[pl.ds(x, 32, stride=16), :].reshape(2, 16, 128).astype(BF16)

    barrier = pltpu.get_barrier_semaphore()
    for step in (-1, 1, -2, 2):
        pl.semaphore_signal(barrier, inc=1, device_id=at(step), device_id_type=MESH)

    for step in (1, ny - 1):
        pl.semaphore_signal(barrier, inc=1, device_id={"gy": lax.rem(gy + step, ny)}, device_id_type=MESH)
    pl.semaphore_wait(barrier, 6)

    def remote(src, dst, n, step):
        return pltpu.make_async_remote_copy(
            src_ref=src, dst_ref=dst, send_sem=send_sem.at[n], recv_sem=recv_sem.at[n],
            device_id=at(step), device_id_type=MESH,
        )

    copies = [
        remote(gsend, xl.at[pl.ds(RIM, 16)], 0, 1),
        remote(gsend, xr.at[pl.ds(0, 16)], 1, -1),
        remote(gsend.at[pl.ds(13, 3)], xl.at[pl.ds(0, RIM)], 2, 2),
        remote(gsend.at[pl.ds(0, 3)], xr.at[pl.ds(16, RIM)], 3, -2),
        remote(ssend.at[pl.ds(3, 3)], sl, 4, 1),
        remote(ssend.at[pl.ds(0, 3)], sr, 5, -1),
    ]
    for copy in copies:
        copy.start()

    for x in range(16):
        field[HALO + x] = g_ref[pl.ds(x, 32, stride=16), :].reshape(4, 8, 128)
        scales[RIM + x] = s_ref[pl.ds(x, 32, stride=16), :]
    for x in (22, 23):
        scales[x] = jnp.zeros((32, 128), F32)
        along[x] = jnp.zeros((4, 8, 128), F32)

    pick = (iota((16, 256), 1) % 16 == iota((16, 256), 0)).astype(BF16)
    level = iota((16, 256), 1) // 16
    wide1 = dot(w1[...], pick)
    row = iota((16, 256), 0)
    for dy in range(3):
        for dx in range(3):
            for f in range(2):
                block = jnp.zeros((16, 256), F32)
                for dz in range(3):
                    k = ((dx * 3 + dy) * 3 + dz) * 2 + f
                    block = jnp.where(level == row + 1 - dz, wide1[k : k + 1, :], block)
                t1[dy * 128 + dx * 32 + f * 16 : dy * 128 + dx * 32 + f * 16 + 16, :] = block.astype(BF16)
        t1[dy * 128 + 96 : dy * 128 + 128, :] = jnp.zeros((32, 256), BF16)

    def one_pair(n, carry):
        blocks = [dot(w2[pl.ds(n * 48 + dz * 16, 16), :], pick) for dz in range(3)]
        for zi in range(16):
            block = jnp.zeros((16, 256), F32)
            for dz in range(3):
                block = jnp.where(level == zi + 1 - dz, blocks[dz], block)
            t2[n, zi * 16 : zi * 16 + 16, :] = block.astype(BF16)
        return carry

    lax.fori_loop(0, 9, one_pair, 0)

    lane = iota((16, 128), 1)
    pick3 = ((iota((8, 128), 1) // 16 == iota((8, 128), 0)) & (iota((8, 128), 0) < 6)).astype(BF16)

    def one_shift(dx, carry):
        blocks = [dot(w3[pl.ds(dx * 48 + dz * 16, 16), :], pick3) for dz in range(3)]
        for zi in range(16):
            block = jnp.zeros((16, 128), F32)
            for dz in range(3):
                block = jnp.where((lane % 16 == zi + 1 - dz) & (lane < 96), blocks[dz], block)
            t3[dx, zi * 16 : zi * 16 + 16, :] = block.astype(BF16)
        return carry

    lax.fori_loop(0, 3, one_shift, 0)

    for f in range(2):
        length = lens[f, 1]
        inverse = tap_rows(length)[1][0:1, :]
        inverse2 = jnp.concatenate([inverse, inverse], axis=1)
        lanes = iota((128, 256), 1)
        target = jnp.where(lanes < 128, lanes, jnp.where(lanes < 131, lanes - 131, lanes - 3))
        away = jnp.abs(iota((128, 256), 0) - target)
        band = jnp.where((away <= RAD) & (lanes < 134), tap(length, away) * inverse2, 0.0)
        own_h[f], own_l[f] = split(band)

        def one_quarter(j, carry):
            for side in range(2):
                place = iota((128, 256), 0)
                k = place % 32
                source = k - HALO if side == 0 else k + 128
                away = jnp.abs(source - target)
                good = (place // 32 == j) & (k < HALO) & (away <= RAD) & (lanes < 134)
                band = jnp.where(good, tap(length, away) * inverse2, 0.0)
                high, low = split(band)
                rim_h[f, j, side * 128 : side * 128 + 128, 0:256] = high
                rim_l[f, j, side * 128 : side * 128 + 128, 0:256] = low
                place1 = iota((128, 128), 0)
                one = (place1 // 32 == j) & (place1 % 32 >= HALO) & (place1 % 32 < HALO + RIM)
                one = one & (iota((128, 128), 1) == place1 % 32 - HALO + RIM * side)
                rim_h[f, j, side * 128 : side * 128 + 128, 256:384] = one.astype(BF16)
                rim_l[f, j, side * 128 : side * 128 + 128, 256:384] = jnp.zeros((128, 128), BF16)
            return carry

        lax.fori_loop(0, 4, one_quarter, 0)

    inv0 = tap_rows(lens[0, 2])[1][0:1, 0:32]
    inv1 = tap_rows(lens[1, 2])[1][0:1, 0:32]
    zo = iota((32, 32), 0)
    zi = iota((32, 32), 1)
    away = jnp.abs(zo - zi)
    both = jnp.where(zo < 16, tap(lens[0, 2], away) * inv0, tap(lens[1, 2], away) * inv1)
    z_high, z_low = split(jnp.where(zo // 16 == zi // 16, both, 0.0))
    zmat[...] = jnp.concatenate([z_high, z_high, z_low], axis=1)

    for copy in copies:
        copy.wait()

    for x in range(HALO):
        left_in = gx * 16 - HALO + x >= 0
        right_in = gx * 16 + 16 + x < nx * 16
        field[x] = jnp.where(left_in, xl[x].astype(F32), 0.0).reshape(4, 8, 128)
        field[HALO + 16 + x] = jnp.where(right_in, xr[x].astype(F32), 0.0).reshape(4, 8, 128)
    for x in range(RIM):
        scales[x] = jnp.where(gx > 0, sl[x].astype(F32), 0.0).reshape(32, 128)
        scales[RIM + 16 + x] = jnp.where(gx < nx - 1, sr[x].astype(F32), 0.0).reshape(32, 128)

    for f in range(2):
        rows = tap_rows(lens[f, 0])[0]

        def one_x(x, carry):
            part = lambda k: field[x + k, 2 * f : 2 * f + 2]
            total = rows[0] * part(RAD)
            for r in range(1, RAD + 1):
                total = total + rows[r] * (part(RAD - r) + part(RAD + r))
            along[x, 2 * f : 2 * f + 2] = total
            return carry

        lax.fori_loop(0, 22, one_x, 0)

    lane32 = iota((32, 128), 1)

    def one_group(g, carry):
        left = jnp.zeros((32, 128), F32)
        right = jnp.zeros((32, 128), F32)
        for j in range(4):
            a = along[4 * g + j].reshape(32, 128)
            s = scales[4 * g + j]
            inside = (lane32 >= 32 * j) & (lane32 < 32 * j + HALO)
            beside = (lane32 >= 32 * j + HALO) & (lane32 < 32 * j + HALO + RIM)
            right = jnp.where(inside, pltpu.roll(a, (32 * j + HALO) % 128, 1), right)
            right = jnp.where(beside, pltpu.roll(s, (32 * j + HALO + RIM) % 128, 1), right)
            left = jnp.where(inside, a if j == 0 else pltpu.roll(a, 32 * j, 1), left)
            left = jnp.where(beside, pltpu.roll(s, 32 * j + HALO, 1), left)
        pack_l[g] = left
        pack_r[g] = right
        return carry

    lax.fori_loop(0, 6, one_group, 0)

    def edge(src, dst, n, to):
        return pltpu.make_async_remote_copy(
            src_ref=src, dst_ref=dst, send_sem=ysend_sem.at[n], recv_sem=yrecv_sem.at[n],
            device_id={"gy": to}, device_id_type=MESH,
        )

    to_right = edge(pack_r, from_l, 0, lax.rem(gy + 1, ny))
    to_left = edge(pack_l, from_r, 1, lax.rem(gy + ny - 1, ny))

    @pl.when(gy < ny - 1)
    def _():
        to_right.start()

    @pl.when(gy > 0)
    def _():
        to_left.start()

    for f in range(2):
        high, low = split(along[:, 2 * f : 2 * f + 2].reshape(384, 128))
        own = dot(high, own_h[f]) + dot(low, own_h[f]) + dot(high, own_l[f])
        smooth[:, f * 16 : f * 16 + 16, :] = own.reshape(24, 16, 256)

    @pl.when(gy < ny - 1)
    def _():
        to_right.wait_send()
        to_left.wait_recv()

    @pl.when(gy > 0)
    def _():
        to_left.wait_send()
        to_right.wait_recv()

    edge_l = jnp.where(gy > 0, from_l[...], 0.0)
    edge_r = jnp.where(gy < ny - 1, from_r[...], 0.0)
    for f in range(2):
        a = jnp.concatenate(
            [edge_l[:, f * 16 : f * 16 + 16].reshape(96, 128), edge_r[:, f * 16 : f * 16 + 16].reshape(96, 128)], axis=1
        )
        high, low = split(a)
        for j in range(4):
            rim = dot(high, rim_h[f, j]) + dot(low, rim_h[f, j]) + dot(high, rim_l[f, j])
            rim = rim.reshape(6, 16, 384)
            for g in range(6):
                x = 4 * g + j
                smooth[x, f * 16 : f * 16 + 16, :] += rim[g, :, 0:256]
                rimscale[x, f * 16 : f * 16 + 16, :] = rim[g, :, 256:384]

    def one_z(x, carry):
        high, low = split(smooth[x])
        z = dot(zmat[...], jnp.concatenate([high, low, high], axis=0))
        scaled[x, :, 0:128] = z[:, 0:128] * scales[x]
        scaled[x, :, 128:256] = z[:, 128:256] * rimscale[x]
        return carry

    lax.fori_loop(0, 24, one_z, 0)

    def one_turn(x, carry):
        turned[16:144, :] = scaled[pl.ds(x, 4), :, 0:128].reshape(128, 128).T
        rim = scaled[pl.ds(x, 4), :, 128:256].reshape(128, 128).T
        turned[13:16, :] = rim[0:3]
        turned[144:147, :] = rim[3:6]
        for dy in range(3):
            lhs[x, :, dy * 128 : dy * 128 + 128] = turned[7 + dy : 7 + dy + ROWS, :].astype(BF16)
        return carry

    turned[0:16, :] = jnp.zeros((16, 128), F32)
    turned[144:160, :] = jnp.zeros((16, 128), F32)
    lax.fori_loop(0, 20, one_turn, 0)

    lane256 = iota((1, 256), 1) % 16
    bias1 = jnp.zeros((1, 256), F32)
    bias2 = jnp.zeros((1, 256), F32)
    for o in range(16):
        bias1 = jnp.where(lane256 == o, b1s[o], bias1)
        bias2 = jnp.where(lane256 == o, b2s[o], bias2)
    y = iota((ROWS, 256), 0) - 8 + gy * 128
    y_in = (y >= 0) & (y < ny * 128)

    def one_first(c, carry):
        v = dot(lhs[pl.ds(c * 4, 4)].reshape(4 * ROWS, 384), t1[...]) + bias1
        v = silu(v).reshape(4, ROWS, 256)
        for n in range(4):
            x = gx * 16 - 2 + c * 4 + n
            h = jnp.where(y_in & (x >= 0) & (x < nx * 16), v[n], 0.0)
            hid1[c * 4 + n, :, 0:256] = pltpu.roll(h, 1, 0).astype(BF16)
            hid1[c * 4 + n, :, 256:512] = h.astype(BF16)
            hid1[c * 4 + n, :, 512:768] = pltpu.roll(h, ROWS - 1, 0).astype(BF16)
        return carry

    lax.fori_loop(0, 5, one_first, 0)

    def one_middle(c, carry):
        v = bias2
        for dx in range(3):
            v = v + dot(hid1[pl.ds(c * 6 + dx, 6)].reshape(6 * ROWS, 768), t2[pl.ds(3 * dx, 3)].reshape(768, 256))
        v = silu(v).reshape(6, ROWS, 256)
        for n in range(6):
            x = gx * 16 - 1 + c * 6 + n
            hid2[c * 6 + n] = jnp.where(y_in & (x >= 0) & (x < nx * 16), v[n], 0.0).astype(BF16)
        return carry

    lax.fori_loop(0, 3, one_middle, 0)

    lane3 = iota((ROWS, 128), 1)
    bias3 = jnp.where(iota((32, 128), 0) < 16, b3s[0], b3s[1])
    for c in range(4):
        p = dot(hid2[c * 4 : c * 4 + 4].reshape(4 * ROWS, 256), t3[0])
        for dx in range(1, 3):
            p = p + dot(hid2[c * 4 + dx : c * 4 + dx + 4].reshape(4 * ROWS, 256), t3[dx])
        p = p.reshape(4, ROWS, 128)
        for n in range(4):
            x = c * 4 + n
            q = jnp.where(lane3 < 32, pltpu.roll(p[n], 1, 0), jnp.where(lane3 < 64, p[n], pltpu.roll(p[n], ROWS - 1, 0)))
            q = q[8:136].T
            total = q[0:32] + q[32:64] + q[64:96] + bias3 + scaled[x + RIM, :, 0:128]
            out_ref[pl.ds(x, 32, stride=16), :] = total


def solution(mesh):
    nx, ny = mesh.shape["gx"], mesh.shape["gy"]

    def per_device(gradient, corr_length, scale, w_first, b_first, w_middle, b_middle, w_last, b_last):
        w1 = jnp.transpose(w_first, (3, 4, 2, 1, 0)).reshape(54, 16)
        w1 = jnp.pad(w1, ((0, 10), (0, 0)))
        w2 = jnp.transpose(w_middle, (3, 4, 2, 1, 0)).reshape(432, 16)
        w3 = jnp.transpose(w_last, (3, 2, 1, 4, 0)).reshape(144, 6)
        w3 = jnp.pad(w3, ((0, 0), (0, 2)))
        smem = pl.BlockSpec(memory_space=pltpu.SMEM)
        vmem = pl.BlockSpec(memory_space=pltpu.VMEM)

        def body(*refs):
            kernel(nx, ny, *refs)

        v = pltpu.VMEM
        out = pl.pallas_call(
            body,
            out_shape=jax.ShapeDtypeStruct((512, 128), F32),
            in_specs=[smem] * 4 + [vmem] * 5,
            out_specs=vmem,
            scratch_shapes=[
                v((16, 2, 16, 128), BF16), v((6, 2, 16, 128), BF16),
                v((HALO, 2, 16, 128), BF16), v((HALO, 2, 16, 128), BF16),
                v((RIM, 2, 16, 128), BF16), v((RIM, 2, 16, 128), BF16),
                v((54, 4, 8, 128), F32), v((24, 4, 8, 128), F32), v((24, 32, 128), F32),
                v((6, 32, 128), F32), v((6, 32, 128), F32), v((6, 32, 128), F32), v((6, 32, 128), F32),
                v((2, 128, 256), BF16), v((2, 128, 256), BF16),
                v((2, 4, 256, 384), BF16), v((2, 4, 256, 384), BF16), v((32, 96), BF16),
                v((24, 32, 256), F32), v((24, 32, 128), F32), v((24, 32, 256), F32),
                v((160, 128), F32), v((20, ROWS, 384), BF16), v((20, ROWS, 768), BF16), v((18, ROWS, 256), BF16),
                v((384, 256), BF16), v((9, 256, 256), BF16), v((3, 256, 128), BF16),
                pltpu.SemaphoreType.DMA((6,)), pltpu.SemaphoreType.DMA((6,)),
                pltpu.SemaphoreType.DMA((2,)), pltpu.SemaphoreType.DMA((2,)),
            ],
            compiler_params=pltpu.CompilerParams(
                collective_id=0, has_side_effects=True, vmem_limit_bytes=56 * 1024 * 1024
            ),
        )(corr_length, b_first, b_middle, b_last, gradient.reshape(512, 128), scale.reshape(512, 128), w1, w2, w3)
        return out.reshape(gradient.shape)

    block = P(None, None, "gx", "gy")
    return jax.shard_map(
        per_device,
        mesh=mesh,
        in_specs=(block, P(), block, P(), P(), P(), P(), P(), P()),
        out_specs=block,
        check_vma=False,
    )
```

time: 347 us -> 53.2 us (0.15)
  the two profiles are of different devices: /device:TPU:47 before, /device:TPU:56 now
where the time goes in v1:
time: 53.2 us; the launch traced here: 53 us
  Pallas kernels  48.3 us (91%)
  local copies, waits for them, and re-layouts  4.66 us (9%)
    pallas_call x1, Pallas kernels, per_device(): pl.pallas_call(body, out_shape=jax.ShapeDtypeStruct((512, 128), F32), in_...  48.3 us
    unnamed x5, local copies, waits for them, and re-layouts  1.68 us

profile of v1, /device:TPU:56, one launch (start us, length us, event | category | flops | bytes accessed | tf_op | source)
XLA Modules:
  0.0 53.0 jit_solution(4631053257349134775)
XLA Ops:
  0.0 0.0 copy-start.1
  0.0 0.7 %copy.13 = bf16[3,3,3,2,16]{4,3,2,1,0:T(2,128)(2,1)S(1)} copy(bf16[3,3,3,2,16]{4,3,1,0,2:T(2,128)(2,1)} %bitcast.14) | data formatting | bytes 3456 | tf_op jit(solution)/shard_map/transpose | solution.py:343
  0.7 0.0 copy-start
  0.8 0.6 %pad.8.refs_6_ = bf16[64,16]{1,0:T(8,128)(2,1)} pad(bf16[54,16]{1,0:T(8,128)(2,1)S(1)} %reshape.20, bf16[]{:T(256)} %constant.2.clone.1), padding=0_10x0_0 | pad | bytes 3778 | tf_op jit(solution)/shard_map/jit(_pad)/pad | solution.py:344
  1.4 0.0 copy-done.1
  1.4 0.1 reshape.22
  1.5 0.1 copy.16
  1.6 0.6 %pad.9.refs_8_ = bf16[144,8]{1,0:T(8,128)(2,1)} pad(bf16[144,6]{1,0:T(8,128)(2,1)S(1)} %copy.16, bf16[]{:T(256)} %constant.2.clone.1), padding=0_0x0_2 | pad | bytes 4034 | tf_op jit(solution)/shard_map/jit(_pad)/pad | solution.py:347
  2.3 0.0 copy-done
  2.3 0.8 %copy.14 = bf16[3,3,3,16,16]{4,3,2,1,0:T(8,128)(2,1)} copy(bf16[3,3,3,16,16]{3,4,1,0,2:T(8,128)(2,1)S(1)} %bitcast.13) | data formatting | bytes 27648 | tf_op jit(solution)/shard_map/transpose | solution.py:345
  3.0 48.3 %shard_map.91 = f32[512,128]{1,0:T(8,128)} custom-call(f32[2,3]{1,0:T(2,128)} %refs_0_.1, f32[16]{0:T(128)} %refs_1_.1, f32[16]{0:T(128)} %refs_2_.1, f32[2]{0:T(128)} %refs_3_.1, f32[512,128]{1,0:T(8,128)} %bitcast.11, f32[512,128]{1,0:T(8,128)} %bitcast.12, bf16[64,16]{1,0:T(8,128)(2,1)} %pad.8.refs_6_, bf16[432,16]{1,0:T(8,128)(2,1)} %bitcast.10, ...), custom_call_target="tpu_custom_call" | custom-call | tf_op jit(solution)/shard_map/pallas_call | solution.py:355
  51.3 1.7 %copy.18 = f32[2,16,16,128]{3,2,1,0:T(8,128)} copy(f32[2,16,16,128]{3,2,1,0:T(8,128)} %bitcast.9) | data formatting | bytes 524288
  (2 shorter events, 0.0 us)
Async XLA Ops:
  0.0 1.4 %copy-start.1 = (bf16[2,16,3,3,3]{1,0,4,3,2:T(2,128)(2,1)S(1)}, bf16[2,16,3,3,3]{1,0,4,3,2:T(2,128)(2,1)}, u32[]{:S(2)}) copy-start(bf16[2,16,3,3,3]{1,0,4,3,2:T(2,128)(2,1)} %param.16) | copy-start | bytes 5188
  0.7 1.5 %copy-start = (bf16[16,16,3,3,3]{1,0,4,3,2:T(8,128)(2,1)S(1)}, bf16[16,16,3,3,3]{1,0,4,3,2:T(8,128)(2,1)}, u32[]{:S(2)}) copy-start(bf16[16,16,3,3,3]{1,0,4,3,2:T(8,128)(2,1)} %param.14) | copy-start | bytes 41476

commit v2 on v1

v2 whole, which is shorter than its diff:
```python
import math

import jax
import jax.numpy as jnp
from jax import lax
from jax.experimental import pallas as pl
from jax.experimental.pallas import tpu as pltpu
from jax.sharding import PartitionSpec as P

RAD = 16
RIM = 3
HALO = RAD + RIM
MESH = pl.DeviceIdType.MESH
F32 = jnp.float32
BF16 = jnp.bfloat16
ROWS = 144
ROOT = math.sqrt(3.0)


def iota(shape, dim):
    return lax.broadcasted_iota(jnp.int32, shape, dim)


def dot(a, b):
    return lax.dot_general(a, b, (((1,), (0,)), ((), ())), preferred_element_type=F32)


def dot_rows(a, b):
    return lax.dot_general(a, b, (((0,), (0,)), ((), ())), preferred_element_type=F32)


def split(value):
    high = value.astype(BF16)
    return high, (value - high.astype(F32)).astype(BF16)


def tap(length, distance):
    s = (ROOT * distance.astype(F32)) / length
    return (1.0 + s) * jnp.exp(-s)


def tap_rows(length):
    rows = [tap(length, jnp.full((8, 128), r, jnp.int32)) for r in range(RAD + 1)]
    total = rows[0] * rows[0]
    for row in rows[1:]:
        total = total + 2.0 * (row * row)
    inverse = 1.0 / jnp.sqrt(total)
    return [row * inverse for row in rows], inverse


def silu(v):
    return v / (1.0 + jnp.exp(-v))


def kernel(
    nx, ny, lens, b1s, b2s, b3s, g_ref, s_ref, w1, w2, w3, out_ref,
    gsend, ssend, xl, xr, sl, sr, field, along, scales, pack_l, pack_r, from_l, from_r,
    own_h, own_l, rim_h, rim_l, zmat, smooth, scaled, turned, lhs, hid1, hid2, t1, t2, t3, flat1, flat3,
    send_sem, recv_sem, ysend_sem, yrecv_sem,
):
    gx = lax.axis_index("gx")
    gy = lax.axis_index("gy")
    at = lambda step: {"gx": lax.rem(gx + nx + step, nx)}

    for f in range(2):
        for x in range(16):
            gsend[f, x] = g_ref[pl.ds(f * 256 + x, 16, stride=16), :].astype(BF16)
        for n, x in enumerate((0, 1, 2, 13, 14, 15)):
            ssend[f, n] = s_ref[pl.ds(f * 256 + x, 16, stride=16), :].astype(BF16)

    barrier = pltpu.get_barrier_semaphore()
    for step in (-1, 1, -2, 2):
        pl.semaphore_signal(barrier, inc=1, device_id=at(step), device_id_type=MESH)

    for step in (1, ny - 1):
        pl.semaphore_signal(barrier, inc=1, device_id={"gy": lax.rem(gy + step, ny)}, device_id_type=MESH)
    pl.semaphore_wait(barrier, 6)

    def remote(src, dst, n, step):
        return pltpu.make_async_remote_copy(
            src_ref=src, dst_ref=dst, send_sem=send_sem.at[n], recv_sem=recv_sem.at[n],
            device_id=at(step), device_id_type=MESH,
        )

    copies = []
    for f in range(2):
        n = 6 * f
        copies.append([
            remote(gsend.at[f], xl.at[f, pl.ds(RIM, 16)], n, 1),
            remote(gsend.at[f], xr.at[f, pl.ds(0, 16)], n + 1, -1),
            remote(gsend.at[f, pl.ds(13, 3)], xl.at[f, pl.ds(0, RIM)], n + 2, 2),
            remote(gsend.at[f, pl.ds(0, 3)], xr.at[f, pl.ds(16, RIM)], n + 3, -2),
            remote(ssend.at[f, pl.ds(3, 3)], sl.at[f], n + 4, 1),
            remote(ssend.at[f, pl.ds(0, 3)], sr.at[f], n + 5, -1),
        ])
    for copy in copies[0] + copies[1]:
        copy.start()

    for x in range(16):
        field[HALO + x] = g_ref[pl.ds(x, 32, stride=16), :].reshape(4, 8, 128)
        scales[RIM + x] = s_ref[pl.ds(x, 32, stride=16), :]
    for x in (22, 23):
        scales[x] = jnp.zeros((32, 128), F32)
        along[x] = jnp.zeros((4, 8, 128), F32)
        scaled[x] = jnp.zeros((32, 256), F32)

    for x in range(20):
        turned[x, 0:16, :] = jnp.zeros((16, 128), F32)
        turned[x, 144:160, :] = jnp.zeros((16, 128), F32)

    pick = (iota((16, 256), 1) % 16 == iota((16, 256), 0)).astype(BF16)
    level = iota((16, 256), 1) // 16
    flat3[...] = jnp.zeros((72, 16), F32)
    for k in range(27):
        flat1[2 * k : 2 * k + 2, :] = w1[k].astype(F32)
        flat3[k // 3 * 8 + k % 3 * 2 : k // 3 * 8 + k % 3 * 2 + 2, :] = w3[k].astype(F32)
    wide1 = dot(flat1[...].astype(BF16), pick)
    row = iota((16, 256), 0)
    for dy in range(3):
        for dx in range(3):
            for f in range(2):
                block = jnp.zeros((16, 256), F32)
                for dz in range(3):
                    k = ((dz * 3 + dx) * 3 + dy) * 2 + f
                    block = jnp.where(level == row + 1 - dz, wide1[k : k + 1, :], block)
                t1[dy * 128 + dx * 32 + f * 16 : dy * 128 + dx * 32 + f * 16 + 16, :] = block.astype(BF16)
        t1[dy * 128 + 96 : dy * 128 + 128, :] = jnp.zeros((32, 256), BF16)

    def one_pair(n, carry):
        blocks = [dot_rows(w2[pl.ds(pl.multiple_of((dz * 9 + n) * 16, 16), 16), :], pick) for dz in range(3)]
        for zi in range(16):
            block = jnp.zeros((16, 256), F32)
            for dz in range(3):
                block = jnp.where(level == zi + 1 - dz, blocks[dz], block)
            t2[n, zi * 16 : zi * 16 + 16, :] = block.astype(BF16)
        return carry

    lax.fori_loop(0, 9, one_pair, 0)

    lane = iota((16, 128), 1)
    pick3 = ((iota((8, 128), 1) // 16 == iota((8, 128), 0)) & (iota((8, 128), 0) < 6)).astype(BF16)

    def one_shift(dx, carry):
        blocks = [dot_rows(flat3[pl.ds(pl.multiple_of((dz * 3 + dx) * 8, 8), 8), :].astype(BF16), pick3) for dz in range(3)]
        for zi in range(16):
            block = jnp.zeros((16, 128), F32)
            for dz in range(3):
                block = jnp.where((lane % 16 == zi + 1 - dz) & (lane < 96), blocks[dz], block)
            t3[dx, zi * 16 : zi * 16 + 16, :] = block.astype(BF16)
        return carry

    lax.fori_loop(0, 3, one_shift, 0)

    for f in range(2):
        length = lens[f, 1]
        inverse = tap_rows(length)[1][0:1, :]
        inverse2 = jnp.concatenate([inverse, inverse], axis=1)
        lanes = iota((128, 256), 1)
        target = jnp.where(lanes < 128, lanes, jnp.where(lanes < 131, lanes - 131, lanes - 3))
        away = jnp.abs(iota((128, 256), 0) - target)
        band = jnp.where((away <= RAD) & (lanes < 134), tap(length, away) * inverse2, 0.0)
        own_h[f], own_l[f] = split(band)

        def one_quarter(j, carry):
            for side in range(2):
                place = iota((128, 256), 0)
                k = place % 32
                source = k - HALO if side == 0 else k + 128
                away = jnp.abs(source - target)
                good = (place // 32 == j) & (k < HALO) & (away <= RAD) & (lanes < 134)
                band = jnp.where(good, tap(length, away) * inverse2, 0.0)
                high, low = split(band)
                rim_h[f, j, side * 128 : side * 128 + 128, 0:256] = high
                rim_l[f, j, side * 128 : side * 128 + 128, 0:256] = low
                place1 = iota((128, 128), 0)
                one = (place1 // 32 == j) & (place1 % 32 >= HALO) & (place1 % 32 < HALO + RIM)
                one = one & (iota((128, 128), 1) == place1 % 32 - HALO + RIM * side)
                rim_h[f, j, side * 128 : side * 128 + 128, 256:384] = one.astype(BF16)
                rim_l[f, j, side * 128 : side * 128 + 128, 256:384] = jnp.zeros((128, 128), BF16)
            return carry

        lax.fori_loop(0, 4, one_quarter, 0)

    away = jnp.abs(iota((16, 16), 0) - iota((16, 16), 1))
    for f in range(2):
        inverse = tap_rows(lens[f, 2])[1][0:1, 0:16]
        high, low = split(tap(lens[f, 2], away) * inverse)
        zmat[f] = jnp.concatenate([high, high, low], axis=1)

    def weighted(rows, f, x, kept):
        part = lambda k: field[x + k, 2 * f : 2 * f + 2]
        total = None
        for r in range(RAD + 1):
            taken = [part(k) for k in sorted({RAD - r, RAD + r}) if kept(x + k)]
            if taken:
                term = rows[r] * (taken[0] if len(taken) == 1 else taken[0] + taken[1])
                total = term if total is None else total + term
        return total

    mine = lambda row: HALO <= row < HALO + 16
    for f in range(2):
        rows = tap_rows(lens[f, 0])[0]
        for x in range(22):
            along[x, 2 * f : 2 * f + 2] = weighted(rows, f, x, mine)

    lane16 = iota((16, 128), 1)

    def edge(src, dst, n, to):
        return pltpu.make_async_remote_copy(
            src_ref=src, dst_ref=dst, send_sem=ysend_sem.at[n], recv_sem=yrecv_sem.at[n],
            device_id={"gy": to}, device_id_type=MESH,
        )

    to_right = [edge(pack_r.at[f], from_l.at[f], f, lax.rem(gy + 1, ny)) for f in range(2)]
    to_left = [edge(pack_l.at[f], from_r.at[f], 2 + f, lax.rem(gy + ny - 1, ny)) for f in range(2)]

    for f in range(2):
        for copy in copies[f]:
            copy.wait()
        for x in range(HALO):
            left_in = gx * 16 - HALO + x >= 0
            right_in = gx * 16 + 16 + x < nx * 16
            field[x, 2 * f : 2 * f + 2] = jnp.where(left_in, xl[f, x].astype(F32), 0.0).reshape(2, 8, 128)
            field[HALO + 16 + x, 2 * f : 2 * f + 2] = jnp.where(right_in, xr[f, x].astype(F32), 0.0).reshape(2, 8, 128)
        for x in range(RIM):
            scales[x, 16 * f : 16 * f + 16] = jnp.where(gx > 0, sl[f, x].astype(F32), 0.0)
            scales[RIM + 16 + x, 16 * f : 16 * f + 16] = jnp.where(gx < nx - 1, sr[f, x].astype(F32), 0.0)
        rows = tap_rows(lens[f, 0])[0]
        for x in range(22):
            along[x, 2 * f : 2 * f + 2] += weighted(rows, f, x, lambda row: not mine(row))

        for g in range(6):
            left = jnp.zeros((16, 128), F32)
            right = jnp.zeros((16, 128), F32)
            for j in range(4):
                a = along[4 * g + j, 2 * f : 2 * f + 2].reshape(16, 128)
                s = scales[4 * g + j, 16 * f : 16 * f + 16]
                inside = (lane16 >= 32 * j) & (lane16 < 32 * j + HALO)
                beside = (lane16 >= 32 * j + HALO) & (lane16 < 32 * j + HALO + RIM)
                right = jnp.where(inside, pltpu.roll(a, (32 * j + HALO) % 128, 1), right)
                right = jnp.where(beside, pltpu.roll(s, (32 * j + HALO + RIM) % 128, 1), right)
                left = jnp.where(inside, a if j == 0 else pltpu.roll(a, 32 * j, 1), left)
                left = jnp.where(beside, pltpu.roll(s, 32 * j + HALO, 1), left)
            pack_l[f, g] = left
            pack_r[f, g] = right

        @pl.when(gy < ny - 1)
        def _():
            to_right[f].start()

        @pl.when(gy > 0)
        def _():
            to_left[f].start()

        high, low = split(along[:, 2 * f : 2 * f + 2].reshape(384, 128))
        own = dot(high, own_h[f]) + dot(low, own_h[f]) + dot(high, own_l[f])
        smooth[:, f * 16 : f * 16 + 16, :] = own.reshape(24, 16, 256)

    for f in range(2):
        @pl.when(gy < ny - 1)
        def _():
            to_right[f].wait_send()
            to_left[f].wait_recv()

        @pl.when(gy > 0)
        def _():
            to_left[f].wait_send()
            to_right[f].wait_recv()

        edge_l = jnp.where(gy > 0, from_l[f], 0.0).reshape(96, 128)
        edge_r = jnp.where(gy < ny - 1, from_r[f], 0.0).reshape(96, 128)
        high, low = split(jnp.concatenate([edge_l, edge_r], axis=1))
        for j in range(4):
            rim = dot(high, rim_h[f, j]) + dot(low, rim_h[f, j]) + dot(high, rim_l[f, j])
            rim = rim.reshape(6, 16, 384)
            for g in range(6):
                x = 4 * g + j
                if x < 22:
                    part = slice(f * 16, f * 16 + 16)
                    high1, low1 = split(smooth[x, part, :] + rim[g, :, 0:256])
                    z = dot(zmat[f], jnp.concatenate([high1, low1, high1], axis=0))
                    scaled[x, part, 0:128] = z[:, 0:128] * scales[x, part]
                    scaled[x, part, 128:256] = z[:, 128:256] * rim[g, :, 256:384]

    def one_turn(x, carry):
        turned[x, 16:144, :] = scaled[pl.ds(x, 4), :, 0:128].reshape(128, 128).T
        rim = scaled[pl.ds(x, 4), :, 128:256].reshape(128, 128).T
        turned[x, 13:16, :] = rim[0:3]
        turned[x, 144:147, :] = rim[3:6]
        for dy in range(3):
            lhs[x, :, dy * 128 : dy * 128 + 128] = turned[x, 7 + dy : 7 + dy + ROWS, :].astype(BF16)
        return carry

    lax.fori_loop(0, 20, one_turn, 0, unroll=5)

    lane256 = iota((1, 256), 1) % 16
    bias1 = jnp.zeros((1, 256), F32)
    bias2 = jnp.zeros((1, 256), F32)
    for o in range(16):
        bias1 = jnp.where(lane256 == o, b1s[o], bias1)
        bias2 = jnp.where(lane256 == o, b2s[o], bias2)
    y = iota((ROWS, 256), 0) - 8 + gy * 128
    y_in = (y >= 0) & (y < ny * 128)

    def one_first(c, carry):
        v = dot(lhs[pl.ds(c * 4, 4)].reshape(4 * ROWS, 384), t1[...]) + bias1
        v = silu(v).reshape(4, ROWS, 256)
        for n in range(4):
            x = gx * 16 - 2 + c * 4 + n
            h = jnp.where(y_in & (x >= 0) & (x < nx * 16), v[n], 0.0)
            hid1[c * 4 + n, :, 0:256] = pltpu.roll(h, 1, 0).astype(BF16)
            hid1[c * 4 + n, :, 256:512] = h.astype(BF16)
            hid1[c * 4 + n, :, 512:768] = pltpu.roll(h, ROWS - 1, 0).astype(BF16)
        return carry

    lax.fori_loop(0, 5, one_first, 0)

    def one_middle(c, carry):
        v = bias2
        for dx in range(3):
            v = v + dot(hid1[pl.ds(c * 6 + dx, 6)].reshape(6 * ROWS, 768), t2[pl.ds(3 * dx, 3)].reshape(768, 256))
        v = silu(v).reshape(6, ROWS, 256)
        for n in range(6):
            x = gx * 16 - 1 + c * 6 + n
            hid2[c * 6 + n] = jnp.where(y_in & (x >= 0) & (x < nx * 16), v[n], 0.0).astype(BF16)
        return carry

    lax.fori_loop(0, 3, one_middle, 0)

    lane3 = iota((ROWS, 128), 1)
    bias3 = jnp.where(iota((32, 128), 0) < 16, b3s[0], b3s[1])
    for c in range(4):
        p = dot(hid2[c * 4 : c * 4 + 4].reshape(4 * ROWS, 256), t3[0])
        for dx in range(1, 3):
            p = p + dot(hid2[c * 4 + dx : c * 4 + dx + 4].reshape(4 * ROWS, 256), t3[dx])
        p = p.reshape(4, ROWS, 128)
        for n in range(4):
            x = c * 4 + n
            q = jnp.where(lane3 < 32, pltpu.roll(p[n], 1, 0), jnp.where(lane3 < 64, p[n], pltpu.roll(p[n], ROWS - 1, 0)))
            q = q[8:136].T
            total = q[0:32] + q[32:64] + q[64:96] + bias3 + scaled[x + RIM, :, 0:128]
            out_ref[pl.ds(x, 32, stride=16), :] = total


def solution(mesh):
    nx, ny = mesh.shape["gx"], mesh.shape["gy"]

    def per_device(gradient, corr_length, scale, w_first, b_first, w_middle, b_middle, w_last, b_last):
        w1 = jnp.transpose(w_first, (2, 3, 4, 1, 0)).reshape(27, 2, 16)
        w2 = jnp.transpose(w_middle, (2, 3, 4, 0, 1)).reshape(432, 16)
        w3 = jnp.transpose(w_last, (2, 3, 4, 0, 1)).reshape(27, 2, 16)
        smem = pl.BlockSpec(memory_space=pltpu.SMEM)
        vmem = pl.BlockSpec(memory_space=pltpu.VMEM)

        def body(*refs):
            kernel(nx, ny, *refs)

        v = pltpu.VMEM
        out = pl.pallas_call(
            body,
            out_shape=jax.ShapeDtypeStruct((512, 128), F32),
            in_specs=[smem] * 4 + [vmem] * 5,
            out_specs=vmem,
            scratch_shapes=[
                v((2, 16, 16, 128), BF16), v((2, 6, 16, 128), BF16),
                v((2, HALO, 16, 128), BF16), v((2, HALO, 16, 128), BF16),
                v((2, RIM, 16, 128), BF16), v((2, RIM, 16, 128), BF16),
                v((54, 4, 8, 128), F32), v((24, 4, 8, 128), F32), v((24, 32, 128), F32),
                v((2, 6, 16, 128), F32), v((2, 6, 16, 128), F32), v((2, 6, 16, 128), F32), v((2, 6, 16, 128), F32),
                v((2, 128, 256), BF16), v((2, 128, 256), BF16),
                v((2, 4, 256, 384), BF16), v((2, 4, 256, 384), BF16), v((2, 16, 48), BF16),
                v((24, 32, 256), F32), v((24, 32, 256), F32),
                v((20, 160, 128), F32), v((20, ROWS, 384), BF16), v((20, ROWS, 768), BF16), v((18, ROWS, 256), BF16),
                v((384, 256), BF16), v((9, 256, 256), BF16), v((3, 256, 128), BF16), v((64, 16), F32), v((72, 16), F32),
                pltpu.SemaphoreType.DMA((12,)), pltpu.SemaphoreType.DMA((12,)),
                pltpu.SemaphoreType.DMA((4,)), pltpu.SemaphoreType.DMA((4,)),
            ],
            compiler_params=pltpu.CompilerParams(
                collective_id=0, has_side_effects=True, vmem_limit_bytes=56 * 1024 * 1024
            ),
        )(corr_length, b_first, b_middle, b_last, gradient.reshape(512, 128), scale.reshape(512, 128), w1, w2, w3)
        return out.reshape(gradient.shape)

    block = P(None, None, "gx", "gy")
    return jax.shard_map(
        per_device,
        mesh=mesh,
        in_specs=(block, P(), block, P(), P(), P(), P(), P(), P()),
        out_specs=block,
        check_vma=False,
    )
```

time: 53.2 us -> 43.2 us (0.81)
  the two profiles are of different devices: /device:TPU:56 before, /device:TPU:40 now
where the time goes in v2:
time: 43.2 us; the launch traced here: 43.1 us
  Pallas kernels  41.4 us (96%)
  local copies, waits for them, and re-layouts  1.67 us (4%)
    pallas_call x1, Pallas kernels, per_device(): pl.pallas_call(body, out_shape=jax.ShapeDtypeStruct((512, 128), F32), in_...  41.4 us
    unnamed x1, local copies, waits for them, and re-layouts  1.67 us

profile of v2, /device:TPU:40, one launch (start us, length us, event | category | flops | bytes accessed | tf_op | source)
XLA Modules:
  0.0 43.1 jit_solution(10183799366431496097)
XLA Ops:
  0.0 41.4 %shard_map.91 = f32[512,128]{1,0:T(8,128)} custom-call(f32[2,3]{1,0:T(2,128)} %refs_0_.1, f32[16]{0:T(128)} %refs_1_.1, f32[16]{0:T(128)} %refs_2_.1, f32[2]{0:T(128)} %refs_3_.1, f32[512,128]{1,0:T(8,128)} %bitcast.13, f32[512,128]{1,0:T(8,128)} %bitcast.14, bf16[27,2,16]{2,1,0:T(2,128)(2,1)} %bitcast.16, bf16[432,16]{1,0:T(8,128)(2,1)} %bitcast.15, ...), custom_call_target="tpu_custom_call" | custom-call | tf_op jit(solution)/shard_map/pallas_call | solution.py:359
  41.4 1.7 %copy.11 = f32[2,16,16,128]{3,2,1,0:T(8,128)} copy(f32[2,16,16,128]{3,2,1,0:T(8,128)} %bitcast.12) | data formatting | bytes 524288

commit v3 on v2

--- a/solution.py
+++ b/solution.py
@@ -49,31 +49,38 @@
 
 
 def silu(v):
-    return v / (1.0 + jnp.exp(-v))
+    half = 0.5 * v
+    return half + half * jnp.tanh(half)
 
 
 def kernel(
-    nx, ny, lens, b1s, b2s, b3s, g_ref, s_ref, w1, w2, w3, out_ref,
+    nx, ny, lens, b1s, b2s, b3s, g_hbm, s_hbm, w1, w2, w3, out_ref,
     gsend, ssend, xl, xr, sl, sr, field, along, scales, pack_l, pack_r, from_l, from_r,
     own_h, own_l, rim_h, rim_l, zmat, smooth, scaled, turned, lhs, hid1, hid2, t1, t2, t3, flat1, flat3,
-    send_sem, recv_sem, ysend_sem, yrecv_sem,
+    g_ref, s_ref, in_sem, send_sem, recv_sem, ysend_sem, yrecv_sem,
 ):
     gx = lax.axis_index("gx")
     gy = lax.axis_index("gy")
     at = lambda step: {"gx": lax.rem(gx + nx + step, nx)}
 
+    take_g = pltpu.make_async_copy(g_hbm, g_ref, in_sem.at[0])
+    take_s = pltpu.make_async_copy(s_hbm, s_ref, in_sem.at[1])
+    take_g.start()
+    take_s.start()
+
+    barrier = pltpu.get_barrier_semaphore()
+    for step in (-1, 1, -2, 2):
+        pl.semaphore_signal(barrier, inc=1, device_id=at(step), device_id_type=MESH)
+
+    for step in (1, ny - 1):
+        pl.semaphore_signal(barrier, inc=1, device_id={"gy": lax.rem(gy + step, ny)}, device_id_type=MESH)
+    take_g.wait()
+    take_s.wait()
     for f in range(2):
         for x in range(16):
             gsend[f, x] = g_ref[pl.ds(f * 256 + x, 16, stride=16), :].astype(BF16)
         for n, x in enumerate((0, 1, 2, 13, 14, 15)):
             ssend[f, n] = s_ref[pl.ds(f * 256 + x, 16, stride=16), :].astype(BF16)
-
-    barrier = pltpu.get_barrier_semaphore()
-    for step in (-1, 1, -2, 2):
-        pl.semaphore_signal(barrier, inc=1, device_id=at(step), device_id_type=MESH)
-
-    for step in (1, ny - 1):
-        pl.semaphore_signal(barrier, inc=1, device_id={"gy": lax.rem(gy + step, ny)}, device_id_type=MESH)
     pl.semaphore_wait(barrier, 6)
 
     def remote(src, dst, n, step):
@@ -313,7 +320,7 @@
             hid1[c * 4 + n, :, 512:768] = pltpu.roll(h, ROWS - 1, 0).astype(BF16)
         return carry
 
-    lax.fori_loop(0, 5, one_first, 0)
+    lax.fori_loop(0, 5, one_first, 0, unroll=True)
 
     def one_middle(c, carry):
         v = bias2
@@ -325,7 +332,7 @@
             hid2[c * 6 + n] = jnp.where(y_in & (x >= 0) & (x < nx * 16), v[n], 0.0).astype(BF16)
         return carry
 
-    lax.fori_loop(0, 3, one_middle, 0)
+    lax.fori_loop(0, 3, one_middle, 0, unroll=True)
 
     lane3 = iota((ROWS, 128), 1)
     bias3 = jnp.where(iota((32, 128), 0) < 16, b3s[0], b3s[1])
@@ -359,7 +366,7 @@
         out = pl.pallas_call(
             body,
             out_shape=jax.ShapeDtypeStruct((512, 128), F32),
-            in_specs=[smem] * 4 + [vmem] * 5,
+            in_specs=[smem] * 4 + [pl.BlockSpec(memory_space=pl.ANY)] * 2 + [vmem] * 3,
             out_specs=vmem,
             scratch_shapes=[
                 v((2, 16, 16, 128), BF16), v((2, 6, 16, 128), BF16),
@@ -372,6 +379,7 @@
                 v((24, 32, 256), F32), v((24, 32, 256), F32),
                 v((20, 160, 128), F32), v((20, ROWS, 384), BF16), v((20, ROWS, 768), BF16), v((18, ROWS, 256), BF16),
                 v((384, 256), BF16), v((9, 256, 256), BF16), v((3, 256, 128), BF16), v((64, 16), F32), v((72, 16), F32),
+                v((512, 128), F32), v((512, 128), F32), pltpu.SemaphoreType.DMA((2,)),
                 pltpu.SemaphoreType.DMA((12,)), pltpu.SemaphoreType.DMA((12,)),
                 pltpu.SemaphoreType.DMA((4,)), pltpu.SemaphoreType.DMA((4,)),
             ],

time: 43.2 us -> 41.7 us (0.965)
  the two profiles are of different devices: /device:TPU:40 before, /device:TPU:56 now
where the time goes in v3:
time: 41.7 us; the launch traced here: 41.5 us
  Pallas kernels  39.8 us (95%)
  local copies, waits for them, and re-layouts  1.67 us (4%)
    pallas_call x1, Pallas kernels, per_device(): pl.pallas_call(body, out_shape=jax.ShapeDtypeStruct((512, 128), F32), in_...  39.8 us
    unnamed x1, local copies, waits for them, and re-layouts  1.67 us

profile of v3, /device:TPU:56, one launch (start us, length us, event | category | flops | bytes accessed | tf_op | source)
XLA Modules:
  0.0 41.5 jit_solution(13849878586714279601)
XLA Ops:
  0.0 39.8 %shard_map.91 = f32[512,128]{1,0:T(8,128)} custom-call(f32[2,3]{1,0:T(2,128)} %refs_0_.1, f32[16]{0:T(128)} %refs_1_.1, f32[16]{0:T(128)} %refs_2_.1, f32[2]{0:T(128)} %refs_3_.1, f32[512,128]{1,0:T(8,128)} %bitcast.13, f32[512,128]{1,0:T(8,128)} %bitcast.14, bf16[27,2,16]{2,1,0:T(2,128)(2,1)} %bitcast.16, bf16[432,16]{1,0:T(8,128)(2,1)} %bitcast.15, ...), custom_call_target="tpu_custom_call" | custom-call | tf_op jit(solution)/shard_map/pallas_call | solution.py:366
  39.8 1.7 %copy.11 = f32[2,16,16,128]{3,2,1,0:T(8,128)} copy(f32[2,16,16,128]{3,2,1,0:T(8,128)} %bitcast.12) | data formatting | bytes 524288

commit v4 on v3

--- a/solution.py
+++ b/solution.py
@@ -298,7 +298,8 @@
             lhs[x, :, dy * 128 : dy * 128 + 128] = turned[x, 7 + dy : 7 + dy + ROWS, :].astype(BF16)
         return carry
 
-    lax.fori_loop(0, 20, one_turn, 0, unroll=5)
+    for x in range(20):
+        one_turn(x, 0)
 
     lane256 = iota((1, 256), 1) % 16
     bias1 = jnp.zeros((1, 256), F32)
@@ -320,19 +321,21 @@
             hid1[c * 4 + n, :, 512:768] = pltpu.roll(h, ROWS - 1, 0).astype(BF16)
         return carry
 
-    lax.fori_loop(0, 5, one_first, 0, unroll=True)
+    for c in range(5):
+        one_first(c, 0)
 
     def one_middle(c, carry):
         v = bias2
         for dx in range(3):
-            v = v + dot(hid1[pl.ds(c * 6 + dx, 6)].reshape(6 * ROWS, 768), t2[pl.ds(3 * dx, 3)].reshape(768, 256))
-        v = silu(v).reshape(6, ROWS, 256)
-        for n in range(6):
-            x = gx * 16 - 1 + c * 6 + n
-            hid2[c * 6 + n] = jnp.where(y_in & (x >= 0) & (x < nx * 16), v[n], 0.0).astype(BF16)
+            v = v + dot(hid1[pl.ds(c * 3 + dx, 3)].reshape(3 * ROWS, 768), t2[pl.ds(3 * dx, 3)].reshape(768, 256))
+        v = silu(v).reshape(3, ROWS, 256)
+        for n in range(3):
+            x = gx * 16 - 1 + c * 3 + n
+            hid2[c * 3 + n] = jnp.where(y_in & (x >= 0) & (x < nx * 16), v[n], 0.0).astype(BF16)
         return carry
 
-    lax.fori_loop(0, 3, one_middle, 0, unroll=True)
+    for c in range(6):
+        one_middle(c, 0)
 
     lane3 = iota((ROWS, 128), 1)
     bias3 = jnp.where(iota((32, 128), 0) < 16, b3s[0], b3s[1])

time: 41.7 us -> 40.3 us (0.966)
  Pallas kernels: 39.8 us -> 38.4 us
    pallas_call x1, Pallas kernels: 39.8 us -> 38.4 us  [per_device(): pl.pallas_call(body, out_shape=jax.ShapeDtypeStruct((512, 128), F32), in_...]
where the time goes in v4:
time: 40.3 us; the launch traced here: 40.1 us
  Pallas kernels  38.4 us (95%)
  local copies, waits for them, and re-layouts  1.67 us (4%)
    pallas_call x1, Pallas kernels, per_device(): pl.pallas_call(body, out_shape=jax.ShapeDtypeStruct((512, 128), F32), in_...  38.4 us
    unnamed x1, local copies, waits for them, and re-layouts  1.67 us

profile of v4, /device:TPU:56, one launch (start us, length us, event | category | flops | bytes accessed | tf_op | source)
XLA Modules:
  0.0 40.1 jit_solution(6907376345368710796)
XLA Ops:
  0.0 38.4 %shard_map.91 = f32[512,128]{1,0:T(8,128)} custom-call(f32[2,3]{1,0:T(2,128)} %refs_0_.1, f32[16]{0:T(128)} %refs_1_.1, f32[16]{0:T(128)} %refs_2_.1, f32[2]{0:T(128)} %refs_3_.1, f32[512,128]{1,0:T(8,128)} %bitcast.13, f32[512,128]{1,0:T(8,128)} %bitcast.14, bf16[27,2,16]{2,1,0:T(2,128)(2,1)} %bitcast.16, bf16[432,16]{1,0:T(8,128)(2,1)} %bitcast.15, ...), custom_call_target="tpu_custom_call" | custom-call | tf_op jit(solution)/shard_map/pallas_call | solution.py:369
  38.4 1.7 %copy.11 = f32[2,16,16,128]{3,2,1,0:T(8,128)} copy(f32[2,16,16,128]{3,2,1,0:T(8,128)} %bitcast.12) | data formatting | bytes 524288
